TPU v7x, 32 devices: a whole 2x2x4 slice. The times are simulated.
32 devices in a mesh: pair: 8 (over z, y), row: 4 (over x, core).
Axes of the slice: x: 2, y: 2, z: 4, core: 2. Of those that a mesh axis runs over, the one named last changes fastest.
Arguments:
- snapshots: float32 [1024, 16384], P('pair', 'row'), may hold values from -50 to 50
- live_rows: int32 [4], P('row'), may hold values from 2048 to 4096, as said below
Outputs:
- rotated: float32 [1024, 16384], P('pair', 'row')
Inputs may be any that keep to these rules, and one draw needn't show every extreme that they name: Row slot s of row index r is live when s < live_rows[r]; every draw has a row index with all 4096 slots live.
All inputs are finite; a program needn't handle non-finite values.
Results may differ from a plain program's by a relative error of at most 0.0003.
Values sent between devices are 32-bit elements; how exact they have to be, the bound alone decides.
A program may use at most 64 MiB of HBM per device.

v0:
```python
import functools

import jax
import jax.numpy as jnp
from jax import lax
from jax.experimental import pallas as pl
from jax.experimental.pallas import tpu as pltpu
from jax.sharding import PartitionSpec as P

ROUNDS = 4
NS_STEPS = 3
EPSILON = 1e-06
MESH = pl.DeviceIdType.MESH
CHUNKS = 4
EARLY = 1
LATE = 1


def own_product(block):
    high, low = halves(block)
    dims = (((1,), (1,)), ((), ()))
    return lax.dot_general(
        jnp.concatenate([high, high], 1),
        jnp.concatenate([high, low], 1),
        dims,
        preferred_element_type=jnp.float32,
    ) + lax.dot_general(low, high, dims, preferred_element_type=jnp.float32)


def eye_mask(rows, columns):
    row = lax.broadcasted_iota(jnp.int32, (rows, columns), 0)
    column = lax.broadcasted_iota(jnp.int32, (rows, columns), 1)
    return row == column


def halves(block):
    high = block.astype(jnp.bfloat16)
    return high, (block - high.astype(jnp.float32)).astype(jnp.bfloat16)


def gram_parts(block):
    high, low = halves(block)
    return lax.dot_general(
        high,
        jnp.concatenate([high, low], 0),
        (((1,), (1,)), ((), ())),
        preferred_element_type=jnp.float32,
    )


def gram_of(parts):
    full = parts.shape[0]
    mixed = parts[:, full:]
    return parts[:, :full] + mixed + mixed.T


def turn_halves(turn):
    high, low = halves(turn)
    return jnp.concatenate([high, high], 1), low


def turned(turn, block):
    wide, low_turn = turn
    high, low = halves(block)
    return jnp.dot(
        wide, jnp.concatenate([high, low], 0), preferred_element_type=jnp.float32
    ) + jnp.dot(low_turn, high, preferred_element_type=jnp.float32)


def norms_of(gram):
    return jnp.sum(jnp.where(eye_mask(*gram.shape), gram, 0.0), axis=0, keepdims=True)


def pack_two(first, second, width):
    lane = lax.broadcasted_iota(jnp.int32, (width, 2 * width), 1)
    line = lax.broadcasted_iota(jnp.int32, (8, 2 * width), 0)
    cross = jnp.where(lane < width, pltpu.roll(second[:width], width, 1), first[:width])
    return cross, jnp.where(line == 0, norms_of(first), norms_of(second))


def pack_one(gram, width):
    part = width // 2
    lane = lax.broadcasted_iota(jnp.int32, (part, 2 * width), 1)
    cross = jnp.where(lane < width, pltpu.roll(gram[:part], width, 1), gram[part:width])
    return cross, jnp.broadcast_to(norms_of(gram), (8, 2 * width))


def rotation_transposed(cross, norms, width):
    full = 2 * width
    lane = lax.broadcasted_iota(jnp.int32, (width, full), 1)
    cross = jnp.where(lane >= width, cross, 0.0)
    upper = jnp.sum(jnp.where(eye_mask(width, full), norms, 0.0), axis=1, keepdims=True)
    spread = norms - upper
    coupling = cross * spread / (spread * spread + 4.0 * cross * cross + upper * norms + EPSILON)
    squares = jnp.sum(jnp.sum(coupling * coupling, axis=1, keepdims=True), axis=0, keepdims=True)
    damping = 1.0 / jnp.sqrt(1.0 + 2.0 * squares)
    corner = jnp.concatenate([coupling, jnp.zeros((width, full), jnp.float32)], 0)
    identity = jnp.where(eye_mask(full, full), 1.0, 0.0)
    return (identity - corner + corner.T) * damping


def orthogonalised(turns):
    for _ in range(NS_STEPS):
        products = [own_product(t) for t in turns]
        turns = [1.5 * t - 0.5 * turned(turn_halves(g), t) for t, g in zip(turns, products)]
    return turns


def kernel(
    pairs, rows, live_ref, x_hbm, out_ref, x_ref, raw, sent0, held1, sent1, held2, sent2, held3, final,
    turn_out, turn_in, singles, doubles, load_sem, raw_send, raw_recv, turn_sem,
    one_send, one_recv, two_send, two_recv, move_send, move_recv, last_send, last_recv,
):
    p, r = lax.axis_index("pair"), lax.axis_index("row")
    plane, y = p // 2, p % 2
    last_plane = pairs // 2 - 1
    partner = 2 * plane + 1 - y
    full, cells = x_ref.shape
    width = full // 2
    half = cells // 2
    step = half // CHUNKS
    first, last = plane == 0, plane == last_plane

    def columns(h, c):
        return pl.ds(pl.multiple_of(h * half + c * step, step), step)

    def load(k):
        part = pl.ds(k * step, step)
        return pltpu.make_async_copy(x_hbm.at[:, part], x_ref.at[:, part], load_sem.at[k])

    for k in range(2 * CHUNKS):
        load(k).start()

    barrier = pltpu.get_barrier_semaphore()
    for k in range(1, 2 * rows):
        other = lax.rem(y * rows + r + k, 2 * rows)
        pl.semaphore_signal(
            barrier, inc=1, device_id=(2 * plane + other // rows, lax.rem(other, rows)), device_id_type=MESH
        )

    @pl.when(plane > 0)
    def _():
        pl.semaphore_signal(barrier, inc=1, device_id=(p - 2, r), device_id_type=MESH)

    @pl.when(plane < last_plane)
    def _():
        pl.semaphore_signal(barrier, inc=1, device_id=(p + 2, r), device_id_type=MESH)

    near = jnp.where(plane > 0, 1, 0) + jnp.where(plane < last_plane, 1, 0)
    pl.semaphore_wait(barrier, 2 * rows - 1 + near)

    def remote(source, target, send_sem, recv_sem, pair_to, row_to=r):
        return pltpu.make_async_remote_copy(
            src_ref=source,
            dst_ref=target,
            send_sem=send_sem,
            recv_sem=recv_sem,
            device_id=(pair_to, row_to),
            device_id_type=MESH,
        )

    def arrived(target, recv_sem):
        pltpu.make_async_copy(target, target, recv_sem).wait()

    def raw_copy(c):
        return remote(
            x_hbm.at[:, columns(1 - y, c)], raw.at[:, pl.ds(c * step, step)], raw_send.at[c], raw_recv.at[c], partner
        )

    def share(buffer, slot, me, count, send_sem, recv_sem, target):
        copies = []
        for k in range(1, count):
            other = lax.rem(me + k, count)
            copy = remote(
                buffer.at[slot, me], buffer.at[slot, me], send_sem.at[slot, k], recv_sem.at[slot, k], *target(other)
            )
            copy.start()
            copies.append(copy)
        return copies

    def total(buffer, slot, count, copies):
        for copy in copies:
            copy.wait()
        result = buffer[slot, 0]
        for k in range(1, count):
            result = result + buffer[slot, k]
        return result

    def share_one(slot, gram):
        cross, tail = pack_one(gram, width)
        singles[slot, r, pl.ds(0, width // 2)] = cross
        singles[slot, r, pl.ds(width // 2, 8)] = tail
        return share(singles, slot, r, rows, one_send, one_recv, lambda other: (p, other))

    def turn_one(slot, copies):
        part = width // 2
        result = total(singles, slot, rows, copies)
        cross = jnp.concatenate([pltpu.roll(result[:part], width, 1), result[:part]], 0)
        return orthogonalised([rotation_transposed(cross, result[part : part + 1], width)])[0]

    def turn_two(slot, grams):
        cross, tail = pack_two(grams[0], grams[1], width)
        me = y * rows + r
        doubles[slot, me, pl.ds(0, width)] = cross
        doubles[slot, me, pl.ds(width, 8)] = tail
        copies = share(
            doubles, slot, me, 2 * rows, two_send, two_recv,
            lambda other: (2 * plane + other // rows, lax.rem(other, rows)),
        )
        result = total(doubles, slot, 2 * rows, copies)
        return orthogonalised([
            rotation_transposed(result[:width], result[width : width + 1], width),
            rotation_transposed(pltpu.roll(result[:width], width, 1), result[width + 1 : width + 2], width),
        ])

    def goes_to(pair, side):
        if side == 0:
            pair_to = jnp.where(pair == 0, 0, jnp.where(pair == pairs - 1, pairs - 1, pair + 1))
            side_to = jnp.where(pair == pairs - 1, 1, 0)
        else:
            pair_to = jnp.where(pair == 0, 1, pair - 1)
            side_to = jnp.where(pair == 0, 0, 1)
        return pair_to, side_to

    def move(number, sent, held, which, side, c):
        pair_to, side_to = goes_to(2 * plane + which, side)
        slot = 2 * lax.rem(pair_to, 2) + side_to
        device = 2 * (pair_to // 2) + y
        part = pl.ds(c * step, step)
        source = sent.at[2 * which + side, :, part]
        target = held.at[slot, :, part]
        recv_sem = move_recv.at[number, slot, c]
        copy = remote(source, target, move_send.at[number, 2 * which + side, c], recv_sem, device)
        return device == p, copy, pltpu.make_async_copy(source, target, recv_sem)

    def start_move(*place):
        local, copy, inside = move(*place)
        if place[3] == place[4]:
            inside.start()
            return

        @pl.when(local)
        def _():
            inside.start()

        @pl.when(jnp.logical_not(local))
        def _():
            copy.start()

    def end_move(*place):
        if place[3] == place[4]:
            return
        local, copy, _ = move(*place)

        @pl.when(jnp.logical_not(local))
        def _():
            copy.wait_send()

    def wait_slots(number, held, slots, c):
        for slot in slots:
            arrived(held.at[slot, :, pl.ds(c * step, step)], move_recv.at[number, slot, c])

    def pair_block(held, which, c):
        return held[pl.ds(2 * which, 2), :, pl.ds(c * step, step)].reshape(full, step)

    live = live_ref[0]

    def masked(block, h, c):
        slot = lax.broadcasted_iota(jnp.int32, (1, step), 1) + (h * half + c * step)
        return jnp.where(slot < live, block, 0.0)

    for c in range(EARLY):
        raw_copy(c).start()
    parts = jnp.zeros((full, 2 * full), jnp.float32)
    for k in range(2 * CHUNKS):
        load(k).wait()
        h, c = k // CHUNKS, k % CHUNKS
        parts = parts + gram_parts(masked(x_ref[:, columns(h, c)], h, c))
    copies = share_one(0, gram_of(parts))
    for c in range(EARLY, CHUNKS - 1):
        raw_copy(c).start()
    turn = turn_one(0, copies)
    turn_out[...] = turn
    turn_copy = remote(turn_out, turn_in, turn_sem.at[0], turn_sem.at[1], partner)
    turn_copy.start()
    for c in range(max(EARLY, CHUNKS - 1), CHUNKS):
        raw_copy(c).start()

    def first_turn(which, turn_parts, block, c):
        sent0[pl.ds(2 * which, 2), :, pl.ds(c * step, step)] = turned(turn_parts, masked(block, y, c)).reshape(
            2, width, step
        )
        for side in range(2):
            for number in range(2):
                @pl.when(which == number)
                def _():
                    start_move(0, sent0, held1, number, side, c)

    own = turn_halves(turn)
    for c in range(CHUNKS):
        first_turn(y, own, x_ref[:, columns(y, c)], c)
    turn_copy.wait()
    other = turn_halves(turn_in[...])
    for c in range(CHUNKS):
        raw_copy(c).wait_recv()
        first_turn(1 - y, other, raw[:, pl.ds(c * step, step)], c)

    def plane_gram(number, held):
        parts = [jnp.zeros((full, 2 * full), jnp.float32)] * 2
        for c in range(CHUNKS):
            wait_slots(number, held, range(4), c)
            parts = [parts[which] + gram_parts(pair_block(held, which, c)) for which in range(2)]
        return [gram_of(part) for part in parts]

    for number, held, sent, held_next in ((0, held1, sent1, held2), (1, held2, sent2, held3)):
        turns = [turn_halves(t) for t in turn_two(number, plane_gram(number, held))]
        for c in range(CHUNKS):
            for which in range(2):
                sent[2 * which : 2 * which + 2, :, pl.ds(c * step, step)] = turned(
                    turns[which], pair_block(held, which, c)
                ).reshape(2, width, step)
                for side in range(2):
                    start_move(number + 1, sent, held_next, which, side, c)

    def hand_back(side, c):
        part = pl.ds(c * step, step)
        return remote(
            held3.at[2 * (1 - y) + side, :, part],
            final.at[side, :, part],
            last_send.at[side, c],
            last_recv.at[side, c],
            partner,
        )

    for c in range(CHUNKS):
        wait_slots(2, held3, (1, 2), c)
        for number in range(2):
            @pl.when(y == number)
            def _():
                hand_back(number, c).start()
    parts = [jnp.zeros((full, 2 * full), jnp.float32)] * 2
    for c in range(CHUNKS):
        wait_slots(2, held3, (0, 3), c)
        if c < LATE:
            for number in range(2):
                @pl.when(y == number)
                def _():
                    hand_back(1 - number, c).start()
        parts = [parts[which] + gram_parts(pair_block(held3, which, c)) for which in range(2)]
    mine, theirs = (jnp.where(y == k, gram_of(parts[0]), gram_of(parts[1])) for k in range(2))
    cross, tail = pack_one(theirs, width)
    singles[2, 0, pl.ds(0, width // 2)] = cross
    singles[2, 0, pl.ds(width // 2, 8)] = tail
    swap = remote(singles.at[2, 0], singles.at[2, 1], turn_sem.at[2], turn_sem.at[3], partner)
    swap.start()
    for c in range(LATE, CHUNKS):
        for number in range(2):
            @pl.when(y == number)
            def _():
                hand_back(1 - number, c).start()
    cross, tail = pack_one(mine, width)
    swap.wait()
    singles[1, r, pl.ds(0, width // 2)] = cross + singles[2, 1, pl.ds(0, width // 2)]
    singles[1, r, pl.ds(width // 2, 8)] = tail + singles[2, 1, pl.ds(width // 2, 8)]
    copies = share(singles, 1, r, rows, one_send, one_recv, lambda other: (p, other))
    own = turn_halves(turn_one(1, copies))
    for c in range(CHUNKS):
        out_ref[:, columns(y, c)] = turned(own, pair_block(held3, y, c))
    for c in range(CHUNKS):
        for side in range(2):
            hand_back(side, c).wait_recv()
        out_ref[:, columns(1 - y, c)] = turned(own, final[:, :, pl.ds(c * step, step)].reshape(full, step))

    for c in range(CHUNKS):
        raw_copy(c).wait_send()
        for which in range(2):
            for side in range(2):
                for number, sent, held in ((0, sent0, held1), (1, sent1, held2), (2, sent2, held3)):
                    end_move(number, sent, held, which, side, c)
        for side in range(2):
            hand_back(side, c).wait_send()


def solution(mesh):
    pairs, rows = mesh.shape["pair"], mesh.shape["row"]

    def body(snapshots, live_rows):
        full, cells = snapshots.shape
        width, half = full // 2, cells // 2
        state = pltpu.VMEM((4, width, half), jnp.float32)
        copies = pltpu.SemaphoreType.DMA
        return pl.pallas_call(
            functools.partial(kernel, pairs, rows),
            out_shape=jax.ShapeDtypeStruct(snapshots.shape, jnp.float32),
            in_specs=[
                pl.BlockSpec(memory_space=pltpu.SMEM),
                pl.BlockSpec(memory_space=pltpu.HBM),
            ],
            out_specs=pl.BlockSpec(memory_space=pltpu.VMEM),
            scratch_shapes=[
                pltpu.VMEM((full, cells), jnp.float32),
                pltpu.VMEM((full, half), jnp.float32),
                state,
                state,
                state,
                state,
                state,
                state,
                pltpu.VMEM((2, width, half), jnp.float32),
                pltpu.VMEM((full, full), jnp.float32),
                pltpu.VMEM((full, full), jnp.float32),
                pltpu.VMEM((3, max(rows, 2), width // 2 + 8, full), jnp.float32),
                pltpu.VMEM((2, 2 * rows, width + 8, full), jnp.float32),
                copies((2 * CHUNKS,)),
                copies((CHUNKS,)),
                copies((CHUNKS,)),
                copies((4,)),
                copies((2, rows)),
                copies((2, rows)),
                copies((2, 2 * rows)),
                copies((2, 2 * rows)),
                copies((3, 4, CHUNKS)),
                copies((3, 4, CHUNKS)),
                copies((2, CHUNKS)),
                copies((2, CHUNKS)),
            ],
            compiler_params=pltpu.CompilerParams(
                collective_id=0, has_side_effects=True, vmem_limit_bytes=48 * 1024 * 1024
            ),
        )(live_rows, snapshots)

    return jax.shard_map(
        body,
        mesh=mesh,
        in_specs=(P("pair", "row"), P("row")),
        out_specs=P("pair", "row"),
        check_vma=False,
    )
```

profile of v0, /device:TPU:0, one launch (start us, length us, event | category | flops | bytes accessed | tf_op | source)
XLA Modules:
  0.0 96.0 jit_solution(6653212538861879505)
XLA Ops:
  0.7 0.0 copy-start
  0.7 1.6 %copy-done = f32[128,4096]{1,0:T(8,128)S(1)} copy-done((f32[128,4096]{1,0:T(8,128)S(1)}, f32[128,4096]{1,0:T(8,128)}, u32[]{:S(2)}) %copy-start) | copy-done | bytes 2097176
  2.2 92.4 %shard_map.28 = f32[128,4096]{1,0:T(8,128)S(1)} custom-call(s32[1]{0:T(128)S(6)} %copy.4.live_ref, f32[128,4096]{1,0:T(8,128)S(1)} %copy-done), custom_call_target="tpu_custom_call" | custom-call | tf_op jit(solution)/shard_map/pallas_call | solution.py:392
  94.6 1.3 %copy.5 = f32[128,4096]{1,0:T(8,128)} copy(f32[128,4096]{1,0:T(8,128)S(1)} %shard_map.28) | data formatting | bytes 4194304
Async XLA Ops:
  0.7 1.6 %copy-start = (f32[128,4096]{1,0:T(8,128)S(1)}, f32[128,4096]{1,0:T(8,128)}, u32[]{:S(2)}) copy-start(f32[128,4096]{1,0:T(8,128)} %x_hbm.1) | copy-start | bytes 6291460
where the time goes:
time: 96.1 us; the launch traced here: 96 us
  Pallas kernels  92.4 us (96%)
  local copies, waits for them, and re-layouts  2.91 us (3%)
    pallas_call x1, Pallas kernels, body(): pl.pallas_call(functools.partial(kernel, pairs, rows), out_shape=jax.Shap...  92.4 us
    unnamed x3, local copies, waits for them, and re-layouts  2.91 us

commit v1 on v0

v1 whole, which is shorter than its diff:
```python
import functools

import jax
import jax.numpy as jnp
from jax import lax
from jax.experimental import pallas as pl
from jax.experimental.pallas import tpu as pltpu
from jax.sharding import PartitionSpec as P

NS_STEPS = 3
EPSILON = 1e-06
MESH = pl.DeviceIdType.MESH
CHUNKS = 8
EARLY = 2
AHEAD = 4
HELD_BACK = 3


def own_product(block):
    high, low = halves(block)
    dims = (((1,), (1,)), ((), ()))
    return lax.dot_general(
        jnp.concatenate([high, high], 1),
        jnp.concatenate([high, low], 1),
        dims,
        preferred_element_type=jnp.float32,
    ) + lax.dot_general(low, high, dims, preferred_element_type=jnp.float32)


def eye_mask(rows, columns):
    row = lax.broadcasted_iota(jnp.int32, (rows, columns), 0)
    column = lax.broadcasted_iota(jnp.int32, (rows, columns), 1)
    return row == column


def halves(block):
    high = block.astype(jnp.bfloat16)
    return high, (block - high.astype(jnp.float32)).astype(jnp.bfloat16)


def gram_parts(block):
    high, low = halves(block)
    return lax.dot_general(
        high,
        jnp.concatenate([high, low], 0),
        (((1,), (1,)), ((), ())),
        preferred_element_type=jnp.float32,
    )


def gram_of(parts):
    full = parts.shape[0]
    mixed = parts[:, full:]
    return parts[:, :full] + mixed + mixed.T


def turn_halves(turn):
    high, low = halves(turn)
    return jnp.concatenate([high, high], 1), low


def turned(turn, block):
    wide, low_turn = turn
    high, low = halves(block)
    return jnp.dot(
        wide, jnp.concatenate([high, low], 0), preferred_element_type=jnp.float32
    ) + jnp.dot(low_turn, high, preferred_element_type=jnp.float32)


def norms_of(gram):
    return jnp.sum(jnp.where(eye_mask(*gram.shape), gram, 0.0), axis=0, keepdims=True)


def pack_two(first, second, width):
    lane = lax.broadcasted_iota(jnp.int32, (width, 2 * width), 1)
    line = lax.broadcasted_iota(jnp.int32, (8, 2 * width), 0)
    cross = jnp.where(lane < width, pltpu.roll(second[:width], width, 1), first[:width])
    return cross, jnp.where(line == 0, norms_of(first), norms_of(second))


def pack_one(gram, width):
    part = width // 2
    lane = lax.broadcasted_iota(jnp.int32, (part, 2 * width), 1)
    cross = jnp.where(lane < width, pltpu.roll(gram[:part], width, 1), gram[part:width])
    return cross, jnp.broadcast_to(norms_of(gram), (8, 2 * width))


def rotation_transposed(cross, norms, width):
    full = 2 * width
    lane = lax.broadcasted_iota(jnp.int32, (width, full), 1)
    cross = jnp.where(lane >= width, cross, 0.0)
    upper = jnp.sum(jnp.where(eye_mask(width, full), norms, 0.0), axis=1, keepdims=True)
    spread = norms - upper
    coupling = cross * spread / (spread * spread + 4.0 * cross * cross + upper * norms + EPSILON)
    squares = jnp.sum(jnp.sum(coupling * coupling, axis=1, keepdims=True), axis=0, keepdims=True)
    damping = 1.0 / jnp.sqrt(1.0 + 2.0 * squares)
    corner = jnp.concatenate([coupling, jnp.zeros((width, full), jnp.float32)], 0)
    identity = jnp.where(eye_mask(full, full), 1.0, 0.0)
    return (identity - corner + corner.T) * damping


def orthogonalised(turns):
    for _ in range(NS_STEPS):
        products = [own_product(t) for t in turns]
        turns = [1.5 * t - 0.5 * turned(turn_halves(g), t) for t, g in zip(turns, products)]
    return turns


def kernel(
    pairs, rows, stop, live_ref, x_hbm, out_ref, x_ref, raw, state1, state2, state3, raw2, final,
    singles, doubles, triples, packed, load_sem, raw_send, raw_recv, fwd_sem,
    one_send, one_recv, two_send, two_recv, three_send, three_recv,
    move_send, move_recv, raw2_send, raw2_recv, last_send, last_recv,
):
    p, r = lax.axis_index("pair"), lax.axis_index("row")
    plane, y = p // 2, p % 2
    last_plane = pairs // 2 - 1
    partner = 2 * plane + 1 - y
    me = y * rows + r
    full, cells = x_ref.shape
    width = full // 2
    part = width // 2
    half = cells // 2
    step = half // CHUNKS
    first, last = plane == 0, plane == last_plane
    pending = []

    def plane_device(other):
        return 2 * plane + other // rows, lax.rem(other, rows)

    barrier = pltpu.get_barrier_semaphore()
    for k in range(1, 2 * rows):
        pl.semaphore_signal(
            barrier, inc=1, device_id=plane_device(lax.rem(me + k, 2 * rows)), device_id_type=MESH
        )

    @pl.when(jnp.logical_not(first))
    def _():
        pl.semaphore_signal(barrier, inc=1, device_id=(p - 2, r), device_id_type=MESH)

    @pl.when(jnp.logical_not(last))
    def _():
        pl.semaphore_signal(barrier, inc=1, device_id=(p + 2, r), device_id_type=MESH)

    def columns(h, c):
        return pl.ds(pl.multiple_of(h * half + c * step, step), step)

    def load(k):
        span = pl.ds(2 * k * step, 2 * step)
        return pltpu.make_async_copy(x_hbm.at[:, span], x_ref.at[:, span], load_sem.at[k])

    for k in range(CHUNKS):
        load(k).start()

    def remote(source, target, send_sem, recv_sem, pair_to, row_to=r):
        return pltpu.make_async_remote_copy(
            src_ref=source,
            dst_ref=target,
            send_sem=send_sem,
            recv_sem=recv_sem,
            device_id=(pair_to, row_to),
            device_id_type=MESH,
        )

    def arrived(target, recv_sem):
        pltpu.make_async_copy(target, target, recv_sem).wait()

    def raw_copy(c):
        return remote(x_hbm.at[:, columns(1 - y, c)], raw.at[c], raw_send.at[c], raw_recv.at[c], partner)

    def raw_start(c):
        raw_copy(c).start()
        pending.append(lambda: raw_copy(c).wait_send())

    def sum_of(buffer, count):
        result = buffer[0]
        for k in range(1, count):
            result = result + buffer[k]
        return result

    live = live_ref[0]

    def masked(block, start, size):
        slot = lax.broadcasted_iota(jnp.int32, (1, size), 1) + start
        return jnp.where(slot < live, block, 0.0)

    def place(which, side):
        if which == 0:
            return jnp.where(first, 0, 2) if side == 0 else jnp.where(first, 2, 5)
        return jnp.where(last, 3, 4) if side == 0 else 1

    def up(number, state, c):
        return remote(
            state.at[4, c], state.at[0, c], move_send.at[number, 0, c], move_recv.at[number, 0, c], p + 2
        )

    def down(number, state, c):
        return remote(
            state.at[5, c], state.at[3, c], move_send.at[number, 1, c], move_recv.at[number, 1, c], p - 2
        )

    def place_turned(number, state, which, turn, block, c):
        result = turned(turn, block)
        if which == 0:
            state[place(0, 0), c] = result[:width]
            state[place(0, 1), c] = result[width:]

            @pl.when(jnp.logical_not(first))
            def _():
                down(number, state, c).start()
        else:
            state[place(1, 0), c] = result[:width]
            state[place(1, 1), c] = result[width:]

            @pl.when(jnp.logical_not(last))
            def _():
                up(number, state, c).start()

    def finish_moves(number, state):
        for c in range(CHUNKS):
            @pl.when(jnp.logical_not(first))
            def _():
                down(number, state, c).wait_send()

            @pl.when(jnp.logical_not(last))
            def _():
                up(number, state, c).wait_send()

    def wait_moved(number, state, c):
        @pl.when(jnp.logical_not(first))
        def _():
            arrived(state.at[0, c], move_recv.at[number, 0, c])

        @pl.when(jnp.logical_not(last))
        def _():
            arrived(state.at[3, c], move_recv.at[number, 1, c])

    def pair_block(state, which, c):
        return state[pl.ds(2 * which, 2), c].reshape(full, step)

    def turn_of(result):
        cross = jnp.concatenate([pltpu.roll(result[:part], width, 1), result[:part]], 0)
        return rotation_transposed(cross, result[part : part + 1], width)

    def turn_two(number, grams):
        cross, tail = pack_two(grams[0], grams[1], width)
        doubles[number, me, pl.ds(0, width)] = cross
        doubles[number, me, pl.ds(width, 8)] = tail
        copies = []
        for k in range(1, 2 * rows):
            copy = remote(
                doubles.at[number, me],
                doubles.at[number, me],
                two_send.at[number, k],
                two_recv.at[number, k],
                *plane_device(lax.rem(me + k, 2 * rows)),
            )
            copy.start()
            copies.append(copy)
        for copy in copies:
            copy.wait_recv()
        pending.append(lambda: [copy.wait_send() for copy in copies])
        result = sum_of(doubles.at[number], 2 * rows)
        return orthogonalised([
            rotation_transposed(result[:width], result[width : width + 1], width),
            rotation_transposed(pltpu.roll(result[:width], width, 1), result[width + 1 : width + 2], width),
        ])

    def finish():
        for wait in pending:
            wait()

    parts = jnp.zeros((full, 2 * full), jnp.float32)
    near = jnp.where(first, 0, 1) + jnp.where(last, 0, 1)
    for k in range(CHUNKS):
        if k == CHUNKS // 2:
            pl.semaphore_wait(barrier, 2 * rows - 1 + near)
            for c in range(EARLY):
                raw_start(c)
        load(k).wait()
        span = pl.ds(2 * k * step, 2 * step)
        parts = parts + gram_parts(masked(x_ref[:, span], 2 * k * step, 2 * step))
    cross, tail = pack_one(gram_of(parts), width)
    singles[r, pl.ds(0, part)] = cross
    singles[r, pl.ds(part, 8)] = tail
    one_copies = []
    for k in range(1, rows):
        copy = remote(singles.at[r], singles.at[r], one_send.at[k], one_recv.at[k], p, lax.rem(r + k, rows))
        copy.start()
        one_copies.append(copy)
    for copy in one_copies:
        copy.wait_recv()
    pending.append(lambda: [copy.wait_send() for copy in one_copies])
    result = sum_of(singles, rows)
    packed[0] = result
    forward = remote(packed.at[0], packed.at[1], fwd_sem.at[0], fwd_sem.at[1], partner)
    forward.start()
    for c in range(EARLY, CHUNKS):
        raw_start(c)
    own = turn_halves(orthogonalised([turn_of(result)])[0])

    def round_zero(turn, mine, c):
        block = x_ref[:, columns(y, c)] if mine else raw[c]
        block = masked(block, y * half + c * step, step)
        for number in range(2):
            @pl.when((y if mine else 1 - y) == number)
            def _():
                place_turned(0, state1, number, turn, block, c)

    for c in range(CHUNKS):
        round_zero(own, True, c)
    forward.wait_recv()
    pending.append(lambda: forward.wait_send())
    other = turn_halves(orthogonalised([turn_of(packed[1])])[0])
    for c in range(CHUNKS):
        raw_copy(c).wait_recv()
        round_zero(other, False, c)

    moves = [(0, c) for c in range(CHUNKS)]
    pending.append(lambda: finish_moves(0, state1))
    if stop == 1:
        for c in range(CHUNKS):
            wait_moved(0, state1, c)
        out_ref[0:64, 0:step] = state1[0, 0]
        return finish()

    parts = [jnp.zeros((full, 2 * full), jnp.float32)] * 2
    for c in range(CHUNKS):
        wait_moved(0, state1, c)
        parts = [parts[which] + gram_parts(pair_block(state1, which, c)) for which in range(2)]
    turns = turn_two(0, [gram_of(q) for q in parts])
    if stop == 2:
        out_ref[0:128, 0:128] = turns[0] + turns[1]
        return finish()
    turns = [turn_halves(t) for t in turns]
    for c in range(CHUNKS):
        for which in range(2):
            place_turned(1, state2, which, turns[which], pair_block(state1, which, c), c)
    pending.append(lambda: finish_moves(1, state2))

    def raw2_copy(c):
        return remote(state2.at[pl.ds(2 * y, 2), c], raw2.at[c], raw2_send.at[c], raw2_recv.at[c], partner)

    parts = [jnp.zeros((full, 2 * full), jnp.float32)] * 2
    for c in range(CHUNKS):
        wait_moved(1, state2, c)
        if c < AHEAD:
            raw2_copy(c).start()
        parts = [parts[which] + gram_parts(pair_block(state2, which, c)) for which in range(2)]
    pending.append(lambda: [raw2_copy(c).wait_send() for c in range(AHEAD)])
    if stop == 3:
        for c in range(AHEAD):
            raw2_copy(c).wait_recv()
        out_ref[0:128, 0:256] = parts[0] + parts[1]
        return finish()
    turns = turn_two(1, [gram_of(q) for q in parts])
    if stop == 4:
        for c in range(AHEAD):
            raw2_copy(c).wait_recv()
        out_ref[0:128, 0:128] = turns[0] + turns[1]
        return finish()

    near_side = jnp.where(y == 0, 0, 1)
    near_slot = jnp.where(y == 0, 2, 1)
    far_slot = jnp.where(y == 0, 3, 0)

    def back_near(c):
        return remote(
            state3.at[near_slot, c], final.at[near_side, c], last_send.at[0, c], last_recv.at[0, c], partner
        )

    def back_far(c):
        return remote(
            state3.at[far_slot, c], final.at[1 - near_side, c], last_send.at[1, c], last_recv.at[1, c], partner
        )

    order = list(range(AHEAD, CHUNKS)) + list(range(AHEAD))
    halves_of = [turn_halves(t) for t in turns]
    for c in order:
        for which in range(2):
            place_turned(2, state3, which, halves_of[which], pair_block(state2, which, c), c)
        if c >= AHEAD:
            back_near(c).start()
    pending.append(lambda: finish_moves(2, state3))
    pending.append(lambda: [back_near(c).wait_send() for c in range(AHEAD, CHUNKS)])

    even_rows = jnp.where(first, turns[0][width:], turns[0][:width])
    taken = turn_halves(jnp.where(y == 1, even_rows, turns[1][width:]))
    for c in range(AHEAD):
        raw2_copy(c).wait_recv()
        final[1 - near_side, c] = turned(taken, raw2[c].reshape(full, step))

    parts = [jnp.zeros((full, 2 * full), jnp.float32)] * 2
    for n, c in enumerate(order):
        wait_moved(2, state3, c)
        if n < CHUNKS - HELD_BACK:
            back_far(c).start()
        parts = [parts[which] + gram_parts(pair_block(state3, which, c)) for which in range(2)]
    if stop == 5:
        out_ref[0:128, 0:256] = parts[0] + parts[1]
        for n, c in enumerate(order):
            if n < CHUNKS - HELD_BACK:
                back_far(c).wait()
        for c in range(AHEAD, CHUNKS):
            back_near(c).wait_recv()
        return finish()
    for which in range(2):
        cross, tail = pack_one(gram_of(parts[which]), width)
        packed[2 + which, pl.ds(0, part)] = cross
        packed[2 + which, pl.ds(part, 8)] = tail

        @pl.when(y == which)
        def _():
            triples[me, pl.ds(0, part)] = cross
            triples[me, pl.ds(part, 8)] = tail

    three_copies = []
    for k in range(1, 2 * rows):
        other_me = lax.rem(me + k, 2 * rows)
        copy = remote(
            packed.at[2 + other_me // rows], triples.at[me], three_send.at[k], three_recv.at[k],
            *plane_device(other_me),
        )
        copy.start()
        three_copies.append(copy)
    for n, c in enumerate(order):
        if n >= CHUNKS - HELD_BACK:
            back_far(c).start()
    pending.append(lambda: [back_far(c).wait_send() for c in range(CHUNKS)])
    for copy in three_copies:
        copy.wait_recv()
    pending.append(lambda: [copy.wait_send() for copy in three_copies])
    own = turn_halves(orthogonalised([turn_of(sum_of(triples, 2 * rows))])[0])
    if stop == 6:
        out_ref[0:128, 0:256] = own[0].astype(jnp.float32)
        for c in range(CHUNKS):
            back_far(c).wait_recv()
        for c in range(AHEAD, CHUNKS):
            back_near(c).wait_recv()
        return finish()
    for c in order:
        out_ref[:, columns(y, c)] = turned(own, pair_block(state3, y, c))
    for c in order:
        if c >= AHEAD:
            back_near(c).wait_recv()
        back_far(c).wait_recv()
        out_ref[:, columns(1 - y, c)] = turned(own, final[:, c].reshape(full, step))
    finish()


def solution(mesh, stop=0):
    pairs, rows = mesh.shape["pair"], mesh.shape["row"]

    def body(snapshots, live_rows):
        full, cells = snapshots.shape
        width, half = full // 2, cells // 2
        step = half // CHUNKS
        state = pltpu.VMEM((6, CHUNKS, width, step), jnp.float32)
        copies = pltpu.SemaphoreType.DMA
        return pl.pallas_call(
            functools.partial(kernel, pairs, rows, stop),
            out_shape=jax.ShapeDtypeStruct(snapshots.shape, jnp.float32),
            in_specs=[
                pl.BlockSpec(memory_space=pltpu.SMEM),
                pl.BlockSpec(memory_space=pltpu.HBM),
            ],
            out_specs=pl.BlockSpec(memory_space=pltpu.VMEM),
            scratch_shapes=[
                pltpu.VMEM((full, cells), jnp.float32),
                pltpu.VMEM((CHUNKS, full, step), jnp.float32),
                state,
                state,
                state,
                pltpu.VMEM((AHEAD, 2, width, step), jnp.float32),
                pltpu.VMEM((2, CHUNKS, width, step), jnp.float32),
                pltpu.VMEM((rows, width // 2 + 8, full), jnp.float32),
                pltpu.VMEM((2, 2 * rows, width + 8, full), jnp.float32),
                pltpu.VMEM((2 * rows, width // 2 + 8, full), jnp.float32),
                pltpu.VMEM((4, width // 2 + 8, full), jnp.float32),
                copies((CHUNKS,)),
                copies((CHUNKS,)),
                copies((CHUNKS,)),
                copies((2,)),
                copies((rows,)),
                copies((rows,)),
                copies((2, 2 * rows)),
                copies((2, 2 * rows)),
                copies((2 * rows,)),
                copies((2 * rows,)),
                copies((3, 2, CHUNKS)),
                copies((3, 2, CHUNKS)),
                copies((AHEAD,)),
                copies((AHEAD,)),
                copies((2, CHUNKS)),
                copies((2, CHUNKS)),
            ],
            compiler_params=pltpu.CompilerParams(
                collective_id=0, has_side_effects=True, vmem_limit_bytes=48 * 1024 * 1024
            ),
        )(live_rows, snapshots)

    return jax.shard_map(
        body,
        mesh=mesh,
        in_specs=(P("pair", "row"), P("row")),
        out_specs=P("pair", "row"),
        check_vma=False,
    )
```

time: 96.1 us -> 87.1 us (0.906)
  Pallas kernels: 92.4 us -> 83.4 us
    pallas_call x1, Pallas kernels: 92.4 us -> 83.4 us  [body(): pl.pallas_call(functools.partial(kernel, pairs, rows, stop), out_shape=ja...]
where the time goes in v1:
time: 87.1 us; the launch traced here: 86.9 us
  Pallas kernels  83.4 us (96%)
  local copies, waits for them, and re-layouts  2.91 us (3%)
    pallas_call x1, Pallas kernels, body(): pl.pallas_call(functools.partial(kernel, pairs, rows, stop), out_shape=ja...  83.4 us
    unnamed x3, local copies, waits for them, and re-layouts  2.91 us

profile of v1, /device:TPU:0, one launch (start us, length us, event | category | flops | bytes accessed | tf_op | source)
XLA Modules:
  0.0 86.9 jit_solution(14549372228576408933)
XLA Ops:
  0.7 0.0 copy-start
  0.7 1.6 %copy-done = f32[128,4096]{1,0:T(8,128)S(1)} copy-done((f32[128,4096]{1,0:T(8,128)S(1)}, f32[128,4096]{1,0:T(8,128)}, u32[]{:S(2)}) %copy-start) | copy-done | bytes 2097176
  2.2 83.4 %shard_map.28 = f32[128,4096]{1,0:T(8,128)S(1)} custom-call(s32[1]{0:T(128)S(6)} %copy.4.live_ref, f32[128,4096]{1,0:T(8,128)S(1)} %copy-done), custom_call_target="tpu_custom_call" | custom-call | tf_op jit(solution)/shard_map/pallas_call | solution.py:460
  85.6 1.3 %copy.5 = f32[128,4096]{1,0:T(8,128)} copy(f32[128,4096]{1,0:T(8,128)S(1)} %shard_map.28) | data formatting | bytes 4194304
Async XLA Ops:
  0.7 1.6 %copy-start = (f32[128,4096]{1,0:T(8,128)S(1)}, f32[128,4096]{1,0:T(8,128)}, u32[]{:S(2)}) copy-start(f32[128,4096]{1,0:T(8,128)} %x_hbm.1) | copy-start | bytes 6291460

commit v2 on v1

--- a/solution.py
+++ b/solution.py
@@ -12,8 +12,12 @@
 MESH = pl.DeviceIdType.MESH
 CHUNKS = 8
 EARLY = 2
-AHEAD = 4
-HELD_BACK = 3
+AHEAD = 3
+AHEAD_FIRST = 2
+RAW_ONE = 4
+RAW_TWO = 2
+RAW_AFTER = (3, 5, 7, 7)
+BACK_FIRST = 4
 
 
 def own_product(block):
@@ -107,10 +111,11 @@
 
 
 def kernel(
-    pairs, rows, stop, live_ref, x_hbm, out_ref, x_ref, raw, state1, state2, state3, raw2, final,
+    pairs, rows, live_ref, x_hbm, out_ref, x_ref, raw, state1, state2, state3, raw2, final, far1, far2, rows_out, rows_in,
     singles, doubles, triples, packed, load_sem, raw_send, raw_recv, fwd_sem,
     one_send, one_recv, two_send, two_recv, three_send, three_recv,
     move_send, move_recv, raw2_send, raw2_recv, last_send, last_recv,
+    far_send, far_recv, rows_send, rows_recv,
 ):
     p, r = lax.axis_index("pair"), lax.axis_index("row")
     plane, y = p // 2, p % 2
@@ -199,25 +204,85 @@
             state.at[5, c], state.at[3, c], move_send.at[number, 1, c], move_recv.at[number, 1, c], p - 2
         )
 
-    def place_turned(number, state, which, turn, block, c):
+    def place_turned(number, state, which, turn, block, c, send=True):
         result = turned(turn, block)
         if which == 0:
             state[place(0, 0), c] = result[:width]
             state[place(0, 1), c] = result[width:]
-
-            @pl.when(jnp.logical_not(first))
-            def _():
-                down(number, state, c).start()
+            if send:
+                @pl.when(jnp.logical_not(first))
+                def _():
+                    down(number, state, c).start()
         else:
             state[place(1, 0), c] = result[:width]
             state[place(1, 1), c] = result[width:]
-
-            @pl.when(jnp.logical_not(last))
-            def _():
-                up(number, state, c).start()
-
-    def finish_moves(number, state):
-        for c in range(CHUNKS):
+            if send:
+                @pl.when(jnp.logical_not(last))
+                def _():
+                    up(number, state, c).start()
+
+    def far_copies(number, state, c):
+        buffer = (far1, far2)[number]
+        lower = remote(
+            state.at[pl.ds(0, 2), c], buffer.at[0, c], far_send.at[number, 0, c], far_recv.at[number, 0, c], p - 2
+        )
+        upper = remote(
+            state.at[pl.ds(2, 2), c], buffer.at[1, c], far_send.at[number, 1, c], far_recv.at[number, 1, c], p + 2
+        )
+        return lower, upper
+
+    def rows_copies(number):
+        lower = remote(
+            rows_out.at[number, 0], rows_in.at[number, 0], rows_send.at[number, 0], rows_recv.at[number, 0], p - 2
+        )
+        upper = remote(
+            rows_out.at[number, 1], rows_in.at[number, 1], rows_send.at[number, 1], rows_recv.at[number, 1], p + 2
+        )
+        return lower, upper
+
+    def both_ways(copies, action):
+        @pl.when(jnp.logical_not(first))
+        def _():
+            getattr(copies[0], action)()
+
+        @pl.when(jnp.logical_not(last))
+        def _():
+            getattr(copies[1], action)()
+
+    def far_start(number, state, c):
+        both_ways(far_copies(number, state, c), "start")
+        pending.append(lambda: both_ways(far_copies(number, state, c), "wait_send"))
+
+    def rows_start(number, turns):
+        rows_out[number, 0] = turns[0][width:]
+        rows_out[number, 1] = turns[1][:width]
+        both_ways(rows_copies(number), "start")
+        pending.append(lambda: both_ways(rows_copies(number), "wait_send"))
+
+    def rows_wait(number):
+        @pl.when(jnp.logical_not(last))
+        def _():
+            arrived(rows_in.at[number, 0], rows_recv.at[number, 0])
+
+        @pl.when(jnp.logical_not(first))
+        def _():
+            arrived(rows_in.at[number, 1], rows_recv.at[number, 1])
+
+    def far_turned(number, state, c):
+        buffer = (far1, far2)[number]
+
+        @pl.when(jnp.logical_not(last))
+        def _():
+            arrived(buffer.at[0, c], far_recv.at[number, 0, c])
+            state[3, c] = turned(turn_halves(rows_in[number, 0]), buffer[0, c].reshape(full, step))
+
+        @pl.when(jnp.logical_not(first))
+        def _():
+            arrived(buffer.at[1, c], far_recv.at[number, 1, c])
+            state[0, c] = turned(turn_halves(rows_in[number, 1]), buffer[1, c].reshape(full, step))
+
+    def finish_moves(number, state, start=0):
+        for c in range(start, CHUNKS):
             @pl.when(jnp.logical_not(first))
             def _():
                 down(number, state, c).wait_send()
@@ -242,7 +307,7 @@
         cross = jnp.concatenate([pltpu.roll(result[:part], width, 1), result[:part]], 0)
         return rotation_transposed(cross, result[part : part + 1], width)
 
-    def turn_two(number, grams):
+    def turn_two(number, grams, between=lambda: None):
         cross, tail = pack_two(grams[0], grams[1], width)
         doubles[number, me, pl.ds(0, width)] = cross
         doubles[number, me, pl.ds(width, 8)] = tail
@@ -257,6 +322,7 @@
             )
             copy.start()
             copies.append(copy)
+        between()
         for copy in copies:
             copy.wait_recv()
         pending.append(lambda: [copy.wait_send() for copy in copies])
@@ -312,54 +378,54 @@
     forward.wait_recv()
     pending.append(lambda: forward.wait_send())
     other = turn_halves(orthogonalised([turn_of(packed[1])])[0])
+    zero = jnp.zeros((full, 2 * full), jnp.float32)
+    parts = [zero, zero]
+
+    def add_gram(parts, state, c):
+        return [parts[which] + gram_parts(pair_block(state, which, c)) for which in range(2)]
+
     for c in range(CHUNKS):
         raw_copy(c).wait_recv()
         round_zero(other, False, c)
-
-    moves = [(0, c) for c in range(CHUNKS)]
+        for j in range(RAW_ONE):
+            if RAW_AFTER[j] == c:
+                wait_moved(0, state1, j)
+                far_start(0, state1, j)
+                parts = add_gram(parts, state1, j)
     pending.append(lambda: finish_moves(0, state1))
-    if stop == 1:
-        for c in range(CHUNKS):
-            wait_moved(0, state1, c)
-        out_ref[0:64, 0:step] = state1[0, 0]
-        return finish()
-
-    parts = [jnp.zeros((full, 2 * full), jnp.float32)] * 2
-    for c in range(CHUNKS):
+    for c in range(RAW_ONE, CHUNKS):
         wait_moved(0, state1, c)
-        parts = [parts[which] + gram_parts(pair_block(state1, which, c)) for which in range(2)]
+        parts = add_gram(parts, state1, c)
     turns = turn_two(0, [gram_of(q) for q in parts])
-    if stop == 2:
-        out_ref[0:128, 0:128] = turns[0] + turns[1]
-        return finish()
+    rows_start(0, turns)
     turns = [turn_halves(t) for t in turns]
-    for c in range(CHUNKS):
+    for c in list(range(RAW_ONE, CHUNKS)) + list(range(RAW_ONE)):
         for which in range(2):
-            place_turned(1, state2, which, turns[which], pair_block(state1, which, c), c)
-    pending.append(lambda: finish_moves(1, state2))
+            place_turned(1, state2, which, turns[which], pair_block(state1, which, c), c, c >= RAW_ONE)
+    pending.append(lambda: finish_moves(1, state2, RAW_ONE))
 
     def raw2_copy(c):
         return remote(state2.at[pl.ds(2 * y, 2), c], raw2.at[c], raw2_send.at[c], raw2_recv.at[c], partner)
 
-    parts = [jnp.zeros((full, 2 * full), jnp.float32)] * 2
+    parts = [zero, zero]
+    rows_wait(0)
     for c in range(CHUNKS):
-        wait_moved(1, state2, c)
-        if c < AHEAD:
+        if c < RAW_ONE:
+            far_turned(0, state2, c)
+        else:
+            wait_moved(1, state2, c)
+        if c < AHEAD_FIRST:
             raw2_copy(c).start()
-        parts = [parts[which] + gram_parts(pair_block(state2, which, c)) for which in range(2)]
+        if c < RAW_TWO:
+            far_start(1, state2, c)
+        parts = add_gram(parts, state2, c)
+
+    def rest_ahead():
+        for c in range(AHEAD_FIRST, AHEAD):
+            raw2_copy(c).start()
+
     pending.append(lambda: [raw2_copy(c).wait_send() for c in range(AHEAD)])
-    if stop == 3:
-        for c in range(AHEAD):
-            raw2_copy(c).wait_recv()
-        out_ref[0:128, 0:256] = parts[0] + parts[1]
-        return finish()
-    turns = turn_two(1, [gram_of(q) for q in parts])
-    if stop == 4:
-        for c in range(AHEAD):
-            raw2_copy(c).wait_recv()
-        out_ref[0:128, 0:128] = turns[0] + turns[1]
-        return finish()
-
+    turns = turn_two(1, [gram_of(q) for q in parts], rest_ahead)
     near_side = jnp.where(y == 0, 0, 1)
     near_slot = jnp.where(y == 0, 2, 1)
     far_slot = jnp.where(y == 0, 3, 0)
@@ -374,36 +440,30 @@
             state3.at[far_slot, c], final.at[1 - near_side, c], last_send.at[1, c], last_recv.at[1, c], partner
         )
 
-    order = list(range(AHEAD, CHUNKS)) + list(range(AHEAD))
+    rows_start(1, turns)
     halves_of = [turn_halves(t) for t in turns]
+    order = [c for c in range(AHEAD, CHUNKS) if c >= RAW_TWO]
+    order += [c for c in range(RAW_TWO, CHUNKS) if c not in order]
+    order += [c for c in range(CHUNKS) if c not in order]
     for c in order:
         for which in range(2):
-            place_turned(2, state3, which, halves_of[which], pair_block(state2, which, c), c)
+            place_turned(2, state3, which, halves_of[which], pair_block(state2, which, c), c, c >= RAW_TWO)
         if c >= AHEAD:
             back_near(c).start()
-    pending.append(lambda: finish_moves(2, state3))
+    pending.append(lambda: finish_moves(2, state3, RAW_TWO))
     pending.append(lambda: [back_near(c).wait_send() for c in range(AHEAD, CHUNKS)])
 
-    even_rows = jnp.where(first, turns[0][width:], turns[0][:width])
-    taken = turn_halves(jnp.where(y == 1, even_rows, turns[1][width:]))
-    for c in range(AHEAD):
-        raw2_copy(c).wait_recv()
-        final[1 - near_side, c] = turned(taken, raw2[c].reshape(full, step))
-
-    parts = [jnp.zeros((full, 2 * full), jnp.float32)] * 2
+    parts = [zero, zero]
+    order = list(range(RAW_TWO)) + [c for c in order if c >= RAW_TWO]
+    rows_wait(1)
     for n, c in enumerate(order):
-        wait_moved(2, state3, c)
-        if n < CHUNKS - HELD_BACK:
+        if c < RAW_TWO:
+            far_turned(1, state3, c)
+        else:
+            wait_moved(2, state3, c)
+        if n < BACK_FIRST:
             back_far(c).start()
-        parts = [parts[which] + gram_parts(pair_block(state3, which, c)) for which in range(2)]
-    if stop == 5:
-        out_ref[0:128, 0:256] = parts[0] + parts[1]
-        for n, c in enumerate(order):
-            if n < CHUNKS - HELD_BACK:
-                back_far(c).wait()
-        for c in range(AHEAD, CHUNKS):
-            back_near(c).wait_recv()
-        return finish()
+        parts = add_gram(parts, state3, c)
     for which in range(2):
         cross, tail = pack_one(gram_of(parts[which]), width)
         packed[2 + which, pl.ds(0, part)] = cross
@@ -423,21 +483,18 @@
         )
         copy.start()
         three_copies.append(copy)
-    for n, c in enumerate(order):
-        if n >= CHUNKS - HELD_BACK:
-            back_far(c).start()
+    for c in order[BACK_FIRST:]:
+        back_far(c).start()
+    even_rows = jnp.where(first, turns[0][width:], turns[0][:width])
+    taken = turn_halves(jnp.where(y == 1, even_rows, turns[1][width:]))
+    for c in range(AHEAD):
+        raw2_copy(c).wait_recv()
+        final[1 - near_side, c] = turned(taken, raw2[c].reshape(full, step))
     pending.append(lambda: [back_far(c).wait_send() for c in range(CHUNKS)])
     for copy in three_copies:
         copy.wait_recv()
     pending.append(lambda: [copy.wait_send() for copy in three_copies])
     own = turn_halves(orthogonalised([turn_of(sum_of(triples, 2 * rows))])[0])
-    if stop == 6:
-        out_ref[0:128, 0:256] = own[0].astype(jnp.float32)
-        for c in range(CHUNKS):
-            back_far(c).wait_recv()
-        for c in range(AHEAD, CHUNKS):
-            back_near(c).wait_recv()
-        return finish()
     for c in order:
         out_ref[:, columns(y, c)] = turned(own, pair_block(state3, y, c))
     for c in order:
@@ -448,7 +505,7 @@
     finish()
 
 
-def solution(mesh, stop=0):
+def solution(mesh):
     pairs, rows = mesh.shape["pair"], mesh.shape["row"]
 
     def body(snapshots, live_rows):
@@ -458,7 +515,7 @@
         state = pltpu.VMEM((6, CHUNKS, width, step), jnp.float32)
         copies = pltpu.SemaphoreType.DMA
         return pl.pallas_call(
-            functools.partial(kernel, pairs, rows, stop),
+            functools.partial(kernel, pairs, rows),
             out_shape=jax.ShapeDtypeStruct(snapshots.shape, jnp.float32),
             in_specs=[
                 pl.BlockSpec(memory_space=pltpu.SMEM),
@@ -473,6 +530,10 @@
                 state,
                 pltpu.VMEM((AHEAD, 2, width, step), jnp.float32),
                 pltpu.VMEM((2, CHUNKS, width, step), jnp.float32),
+                pltpu.VMEM((2, RAW_ONE, 2, width, step), jnp.float32),
+                pltpu.VMEM((2, RAW_TWO, 2, width, step), jnp.float32),
+                pltpu.VMEM((2, 2, width, full), jnp.float32),
+                pltpu.VMEM((2, 2, width, full), jnp.float32),
                 pltpu.VMEM((rows, width // 2 + 8, full), jnp.float32),
                 pltpu.VMEM((2, 2 * rows, width + 8, full), jnp.float32),
                 pltpu.VMEM((2 * rows, width // 2 + 8, full), jnp.float32),
@@ -493,11 +554,15 @@
                 copies((AHEAD,)),
                 copies((2, CHUNKS)),
                 copies((2, CHUNKS)),
+                copies((2, 2, CHUNKS)),
+                copies((2, 2, CHUNKS)),
+                copies((2, 2)),
+                copies((2, 2)),
             ],
             compiler_params=pltpu.CompilerParams(
                 collective_id=0, has_side_effects=True, vmem_limit_bytes=48 * 1024 * 1024
             ),
-        )(live_rows, snapshots)
+        )(live_rows, pltpu.with_memory_space_constraint(snapshots, pltpu.HBM))
 
     return jax.shard_map(
         body,

time: 87.1 us -> 81.8 us (0.939)
  Pallas kernels: 83.4 us -> 79.7 us
  local copies, waits for them, and re-layouts: 2.91 us -> 1.32 us
    pallas_call x1, Pallas kernels: 83.4 us -> 79.7 us  [body(): pl.pallas_call(functools.partial(kernel, pairs, rows), out_shape=jax.Shap...]
    unnamed x3 -> x1, local copies, waits for them, and re-layouts: 2.91 us -> 1.32 us
where the time goes in v2:
time: 81.8 us; the launch traced here: 81.7 us
  Pallas kernels  79.7 us (97%)
  local copies, waits for them, and re-layouts  1.32 us (2%)
    pallas_call x1, Pallas kernels, body(): pl.pallas_call(functools.partial(kernel, pairs, rows), out_shape=jax.Shap...  79.7 us

profile of v2, /device:TPU:0, one launch (start us, length us, event | category | flops | bytes accessed | tf_op | source)
XLA Modules:
  0.0 81.7 jit_solution(2211310585540965991)
XLA Ops:
  0.7 79.7 %shard_map.28 = f32[128,4096]{1,0:T(8,128)S(1)} custom-call(s32[1]{0:T(128)S(6)} %copy.4.live_ref, f32[128,4096]{1,0:T(8,128)} %x_hbm.1), custom_call_target="tpu_custom_call" | custom-call | tf_op jit(solution)/shard_map/pallas_call | solution.py:517
  80.4 1.3 %copy.5 = f32[128,4096]{1,0:T(8,128)} copy(f32[128,4096]{1,0:T(8,128)S(1)} %shard_map.28) | data formatting | bytes 4194304
